TPU v7x, 256 devices: a whole 4x4x8 slice. The times are simulated.
256 devices in a mesh: dp: 16 (over z, core), expert: 16 (over y, x).
Axes of the slice: x: 4, y: 4, z: 8, core: 2. Of those that a mesh axis runs over, the one named last changes fastest.
Arguments:
- tokens: bfloat16 [16384, 2048], P(('dp', 'expert')), parts along dimension 0, may hold values from -6 to 6
- router_weight: bfloat16 [2048, 16], replicated, may hold values from -0.125 to 0.125
- gate_weight: bfloat16 [16, 2048, 768], P('expert'), may hold values from -0.125 to 0.125
- up_weight: bfloat16 [16, 2048, 768], P('expert'), may hold values from -0.125 to 0.125
- down_weight: bfloat16 [16, 768, 2048], P('expert'), may hold values from -0.21875 to 0.21875
- routing: int32 [16384, 4], P(('dp', 'expert')), parts along dimension 0, may hold values from 0 to 15, as said below
- priority: int32 [256, 256], P(('dp', 'expert')), parts along dimension 0, may hold values from 0 to 255, each once within a row
- hot_list: int32 [32], P('dp'), parts along dimension 0, may hold values from 0 to 15, as said below
Outputs:
- mixed: bfloat16 [16384, 2048], P(('dp', 'expert')), parts along dimension 0
There are 16 independent parts, one for each index of `dp`. A program takes and returns all parts, laid end to end along the dimension named above; an argument that names none is the same for every part. Nothing has to cross between parts.
Inputs may be any that keep to these rules, and one draw needn't show every extreme that they name: `routing`: each token names 4 different experts. `priority`: each row is a permutation. `hot_list`: 2 different experts.
All inputs are finite; a program needn't handle non-finite values.
Results may differ from a plain program's by a relative error of at most 0.0085.
Values may be sent and summed in bfloat16 or wider, within the bound.
A program may use at most 64 MiB of HBM per device.

v0:
```python
import jax
import jax.numpy as jnp
from jax import lax
from jax.sharding import PartitionSpec as P


def expert_swiglu(inputs, gate_mat, up_mat, down_mat):
    gate_part = jnp.dot(inputs, gate_mat, preferred_element_type=jnp.float32)
    up_part = jnp.dot(inputs, up_mat, preferred_element_type=jnp.float32)
    hidden = (jax.nn.silu(gate_part) * up_part).astype(jnp.bfloat16)
    return jnp.dot(hidden, down_mat, preferred_element_type=jnp.float32).astype(jnp.bfloat16)


def shards(tokens, router_weight, gate_weight, up_weight, down_weight, routing, priority, hot_list):
    devices_n = lax.axis_size("expert")
    tok_count, width = tokens.shape
    top_count = routing.shape[1]
    slot_count = tok_count * top_count
    capacity = min(tok_count, 3 * slot_count // (2 * devices_n))
    logits = jnp.dot(tokens, router_weight, preferred_element_type=jnp.float32)
    chosen = jnp.take_along_axis(logits, routing, axis=1)
    sigmas = jax.nn.sigmoid(chosen)
    weights = sigmas / jnp.sum(sigmas, axis=1, keepdims=True)
    hot_flag = jnp.any(routing[:, :, None] == hot_list[None, None, :], axis=2)
    slot_expert = routing.reshape(-1)
    slot_order = priority[0]
    same_expert = slot_expert[:, None] == slot_expert[None, :]
    earlier = slot_order[None, :] < slot_order[:, None]
    ranks = jnp.sum((same_expert & earlier).astype(jnp.int32), axis=1)
    sending = jnp.logical_not(hot_flag.reshape(-1)) & (ranks < capacity)
    cell_index = slot_expert * capacity + ranks
    cell_count = devices_n * capacity
    cells = lax.broadcasted_iota(jnp.int32, (cell_count, slot_count), 0)
    placed = (cells == cell_index[None, :]) & sending[None, :]
    dispatch = jnp.sum(
        placed.reshape(cell_count, tok_count, top_count).astype(jnp.float32), axis=2
    ).astype(jnp.bfloat16)
    outbound = jnp.dot(dispatch, tokens, preferred_element_type=jnp.float32).astype(jnp.bfloat16)
    outbound = outbound.reshape(devices_n, capacity, width)
    received = lax.all_to_all(outbound, "expert", split_axis=0, concat_axis=0, tiled=True)
    flat_rows = received.reshape(-1, width)
    answer = expert_swiglu(flat_rows, gate_weight[0], up_weight[0], down_weight[0]).reshape(
        received.shape
    )
    returned = lax.all_to_all(answer, "expert", split_axis=0, concat_axis=0, tiled=True)
    returned_flat = returned.reshape(cell_count, width)
    safe_cell = jnp.where(sending, cell_index, 0)
    slot_answer = jnp.take(returned_flat, safe_cell, axis=0).reshape(tok_count, top_count, width)
    slot_weight = jnp.where(sending.reshape(tok_count, top_count), weights, 0.0)
    mixed = jnp.sum(slot_weight[:, :, None] * slot_answer.astype(jnp.float32), axis=1)
    owners = lax.broadcasted_iota(jnp.int32, (devices_n, tok_count, top_count), 0)
    picked = (routing[None, :, :] == owners) & hot_flag[None, :, :]
    asked = jnp.any(picked, axis=2)
    outgoing = jnp.where(asked[:, :, None], tokens[None, :, :], jnp.zeros((), jnp.bfloat16))
    received = lax.all_to_all(outgoing, "expert", split_axis=0, concat_axis=0, tiled=True)
    flat_rows = received.reshape(-1, width)
    answer = expert_swiglu(flat_rows, gate_weight[0], up_weight[0], down_weight[0]).reshape(
        received.shape
    )
    answers = lax.all_to_all(answer, "expert", split_axis=0, concat_axis=0, tiled=True)
    hot_answers = jnp.take(answers, hot_list, axis=0)
    hot_share = jnp.sum(
        jnp.where(routing[None, :, :] == hot_list[:, None, None], weights[None, :, :], 0.0), axis=2
    )
    mixed = mixed + jnp.sum(hot_share[:, :, None] * hot_answers.astype(jnp.float32), axis=0)
    return mixed.astype(jnp.bfloat16)


def solution(mesh):
    return jax.shard_map(
        shards,
        mesh=mesh,
        in_specs=(
            P(("dp", "expert"), None),
            P(),
            P("expert", None, None),
            P("expert", None, None),
            P("expert", None, None),
            P(("dp", "expert"), None),
            P(("dp", "expert"), None),
            P("dp"),
        ),
        out_specs=P(("dp", "expert"), None),
        check_vma=False,
    )
```

profile of v0, /device:TPU:32, one launch (start us, length us, event | category | flops | bytes accessed | tf_op | source)
XLA Modules:
  0.0 195.9 jit_solution(10542164263017563908)
XLA Ops:
  0.0 0.0 copy-start
  0.0 0.0 copy-start.2
  0.0 0.9 copy.28
  0.9 0.1 eq.61
  1.0 1.0 convert_reduce_fusion.1
  2.0 0.1 reduce_sum.59
  2.1 0.1 copy.29
  2.2 0.8 compare_reduce_fusion
  3.0 0.7 compare_and_fusion.1
  3.7 0.1 convert_reduce_fusion
  3.8 2.7 %convolution_convert_fusion.1 = bf16[384,2048]{1,0:T(8,128)(2,1)} fusion(bf16[64,2048]{1,0:T(8,128)(2,1)} %param.8, bf16[384,64]{0,1:T(8,128)(2,1)S(1)} %convert_reduce_fusion), kind=kOutput, calls=%fused_computation.18 | convolution fusion | flops 101449728 | bytes 1884160 | tf_op jit(solution)/shard_map/dot_general | solution.py:38
  6.5 7.1 %all-to-all-start = ((bf16[16,24,2048]{2,1,0:T(8,128)(2,1)}), bf16[16,24,2048]{2,1,0:T(8,128)(2,1)}, u32[]{:S(2)}, u32[]{:S(2)}) async-start(bf16[16,24,2048]{2,1,0:T(8,128)(2,1)} %bitcast.48), calls=%async_computation | async-start | bytes 3145728 | tf_op jit(solution)/shard_map/all_to_all | solution.py:40
  13.6 0.0 copy-done.2
  13.7 0.0 copy-done.1
  13.7 2.3 %broadcast_select_fusion = bf16[16,64,2048]{2,1,0:T(8,128)(2,1)} fusion(pred[16,64]{1,0:T(8,128)(4,1)S(1)} %fusion.30, bf16[64,2048]{1,0:T(8,128)(2,1)S(1)} %copy-done.1), kind=kLoop, calls=%fused_computation.3 | loop fusion | flops 2097152 | bytes 4457472 | tf_op jit(solution)/shard_map/jit(_where)/select_n | solution.py:54
  16.0 22.2 %all-to-all-done = bf16[16,24,2048]{2,1,0:T(8,128)(2,1)} async-done(((bf16[16,24,2048]{2,1,0:T(8,128)(2,1)}), bf16[16,24,2048]{2,1,0:T(8,128)(2,1)}, u32[]{:S(2)}, u32[]{:S(2)}) %all-to-all-start) | async-done | bytes 1572896 | tf_op jit(solution)/shard_map/all_to_all | solution.py:40
  38.2 4.5 %all-to-all-start.2 = ((bf16[16,64,2048]{2,1,0:T(8,128)(2,1)}), bf16[16,64,2048]{2,1,0:T(8,128)(2,1)}, u32[]{:S(2)}, u32[]{:S(2)}) async-start(bf16[16,64,2048]{2,1,0:T(8,128)(2,1)} %broadcast_select_fusion), calls=%async_computation.2 | async-start | bytes 8388608 | tf_op jit(solution)/shard_map/all_to_all | solution.py:55
  42.7 4.8 %fusion.9 = f32[384,768]{1,0:T(8,128)} fusion(bf16[384,2048]{1,0:T(8,128)(2,1)} %bitcast.3, bf16[1,2048,768]{2,1,0:T(8,128)(2,1)} %param.10), kind=kOutput, calls=%fused_computation.14 | convolution fusion | flops 1207959552 | bytes 5898240 | tf_op jit(solution)/shard_map/dot_general | solution.py:8
  47.5 0.0 copy-done
  47.5 6.9 %fusion.11 = bf16[384,2048]{1,0:T(8,128)(2,1)} fusion(bf16[1,768,2048]{2,1,0:T(8,128)(2,1)S(1)} %copy-done, bf16[384,2048]{1,0:T(8,128)(2,1)} %bitcast.3, bf16[1,2048,768]{2,1,0:T(8,128)(2,1)} %param.11, f32[384,768]{1,0:T(8,128)} %fusion.9), kind=kOutput, calls=%fused_computation.17 | convolution fusion | flops 2418475008 | bytes 10616832 | tf_op jit(solution)/shard_map/dot_general | solution.py:11
  54.4 47.7 %all-to-all-done.2 = bf16[16,64,2048]{2,1,0:T(8,128)(2,1)} async-done(((bf16[16,64,2048]{2,1,0:T(8,128)(2,1)}), bf16[16,64,2048]{2,1,0:T(8,128)(2,1)}, u32[]{:S(2)}, u32[]{:S(2)}) %all-to-all-start.2) | async-done | bytes 4194336 | tf_op jit(solution)/shard_map/all_to_all | solution.py:55
  102.1 4.4 %all-to-all-start.1 = ((bf16[16,24,2048]{2,1,0:T(8,128)(2,1)}), bf16[16,24,2048]{2,1,0:T(8,128)(2,1)}, u32[]{:S(2)}, u32[]{:S(2)}) async-start(bf16[16,24,2048]{2,1,0:T(8,128)(2,1)} %bitcast.50), calls=%async_computation.1 | async-start | bytes 3145728 | tf_op jit(solution)/shard_map/all_to_all | solution.py:45
  106.5 8.3 %fusion.3 = f32[1024,768]{1,0:T(8,128)} fusion(bf16[1024,2048]{1,0:T(8,128)(2,1)} %bitcast.11, bf16[1,2048,768]{2,1,0:T(8,128)(2,1)} %param.11), kind=kOutput, calls=%fused_computation.8 | convolution fusion | flops 3221225472 | bytes 10485760 | tf_op jit(solution)/shard_map/dot_general | solution.py:9
  114.9 12.3 %convolution_convert_fusion = bf16[1024,2048]{1,0:T(8,128)(2,1)} fusion(bf16[1,768,2048]{2,1,0:T(8,128)(2,1)S(1)} %copy-done, f32[1024,768]{1,0:T(8,128)} %fusion.3, bf16[1024,2048]{1,0:T(8,128)(2,1)} %bitcast.11, bf16[1,2048,768]{2,1,0:T(8,128)(2,1)} %param.10), kind=kOutput, calls=%fused_computation.4 | convolution fusion | flops 6449266688 | bytes 17825792 | tf_op jit(solution)/shard_map/dot_general | solution.py:11
  127.2 0.9 all-to-all-done.1
  128.2 6.4 %all-to-all-start.3 = ((bf16[16,64,2048]{2,1,0:T(8,128)(2,1)}), bf16[16,64,2048]{2,1,0:T(8,128)(2,1)}, u32[]{:S(2)}, u32[]{:S(2)}) async-start(bf16[16,64,2048]{2,1,0:T(8,128)(2,1)} %bitcast.49), calls=%async_computation.3 | async-start | bytes 8388608 | tf_op jit(solution)/shard_map/all_to_all | solution.py:60
  134.5 0.1 copy.35
  134.6 0.1 not.24
  134.8 0.1 copy.36
  134.9 0.1 mul.54
  135.0 0.1 copy.30
  135.1 0.1 reshape.199
  135.2 0.0 copy-done.3
  135.2 0.2 fusion.35
  135.4 2.0 %gather_fusion.2 = f32[256]{0:T(256)S(1)} fusion(f32[64,16]{0,1:T(8,128)S(1)} %fusion.35, s32[256]{0:T(256)S(1)} %reshape.199), kind=kCustom, calls=%fused_computation.2 | custom fusion | bytes 4096 | tf_op jit(solution)/shard_map/jit(take_along_axis)/gather | solution.py:21
  137.4 0.1 reshape.202
  137.5 0.1 copy.31
  137.7 0.1 copy.32
  137.8 0.1 copy.34
  137.9 0.0 copy-done.4
  137.9 0.1 select_reduce_fusion
  138.0 5.0 %gather_fusion = bf16[256,2048]{1,0:T(8,128)(2,1)} fusion(bf16[384,2048]{1,0:T(8,128)(2,1)} %bitcast.8, s32[1024]{0:T(1024)S(1)} %pad_clamp_fusion.1), kind=kCustom, calls=%fused_computation | custom fusion | bytes 2098176 | tf_op jit(solution)/shard_map/jit(_take)/gather | solution.py:48
  143.1 2.2 %gather.16 = bf16[64,4,2048]{2,1,0:T(4,128)(2,1)} reshape(bf16[256,2048]{1,0:T(8,128)(2,1)} %gather_fusion) | data formatting | bytes 2097152 | tf_op jit(solution)/shard_map/jit(_take)/gather | solution.py:48
  145.3 4.7 %multiply_reduce_fusion = f32[64,2048]{1,0:T(8,128)} fusion(bf16[64,4,2048]{2,1,0:T(4,128)(2,1)} %gather.16, f32[64,4]{1,0:T(8,128)S(1)} %copy.32, pred[64,4]{1,0:T(8,128)(4,1)S(1)} %copy.34), kind=kLoop, calls=%fused_computation.19 | loop fusion | flops 1966080 | bytes 1574144 | tf_op jit(solution)/shard_map/reduce_sum | solution.py:50
  150.0 39.3 %all-to-all-done.3 = bf16[16,64,2048]{2,1,0:T(8,128)(2,1)} async-done(((bf16[16,64,2048]{2,1,0:T(8,128)(2,1)}), bf16[16,64,2048]{2,1,0:T(8,128)(2,1)}, u32[]{:S(2)}, u32[]{:S(2)}) %all-to-all-start.3) | async-done | bytes 4194336 | tf_op jit(solution)/shard_map/all_to_all | solution.py:60
  189.3 3.6 %gather_fusion.1 = bf16[2,64,2048]{2,1,0:T(8,128)(2,1)} fusion(bf16[16,64,2048]{2,1,0:T(8,128)(2,1)} %all-to-all-done.3, s32[1024]{0:T(1024)S(1)} %pad_clamp_fusion), kind=kCustom, calls=%fused_computation.1 | custom fusion | bytes 1048584 | tf_op jit(solution)/shard_map/jit(_take)/gather | solution.py:61
  192.8 1.3 multiply_reduce_fusion.1
  194.1 1.8 add_convert_fusion
  (13 shorter events, 0.1 us)
Async XLA Ops:
  0.0 47.5 %copy-start = (bf16[1,768,2048]{2,1,0:T(8,128)(2,1)S(1)}, bf16[1,768,2048]{2,1,0:T(8,128)(2,1)}, u32[]{:S(2)}) copy-start(bf16[1,768,2048]{2,1,0:T(8,128)(2,1)} %param.12) | copy-start | bytes 9437188
  0.0 13.6 %copy-start.2 = (s32[64,4]{0,1:T(4,128)S(1)}, s32[64,4]{0,1:T(4,128)}, u32[]{:S(2)}) copy-start(s32[64,4]{0,1:T(4,128)} %param.13) | copy-start | bytes 3076
  0.0 13.6 %copy-start.1 = (bf16[64,2048]{1,0:T(8,128)(2,1)S(1)}, bf16[64,2048]{1,0:T(8,128)(2,1)}, u32[]{:S(2)}) copy-start(bf16[64,2048]{1,0:T(8,128)(2,1)} %param.8) | copy-start | bytes 786436
  6.5 31.7 %all-to-all-start = ((bf16[16,24,2048]{2,1,0:T(8,128)(2,1)}), bf16[16,24,2048]{2,1,0:T(8,128)(2,1)}, u32[]{:S(2)}, u32[]{:S(2)}) async-start(bf16[16,24,2048]{2,1,0:T(8,128)(2,1)} %bitcast.48), calls=%async_computation | async-start | bytes 3145728 | tf_op jit(solution)/shard_map/all_to_all | solution.py:40
  38.2 63.9 %all-to-all-start.2 = ((bf16[16,64,2048]{2,1,0:T(8,128)(2,1)}), bf16[16,64,2048]{2,1,0:T(8,128)(2,1)}, u32[]{:S(2)}, u32[]{:S(2)}) async-start(bf16[16,64,2048]{2,1,0:T(8,128)(2,1)} %broadcast_select_fusion), calls=%async_computation.2 | async-start | bytes 8388608 | tf_op jit(solution)/shard_map/all_to_all | solution.py:55
  102.1 26.0 %all-to-all-start.1 = ((bf16[16,24,2048]{2,1,0:T(8,128)(2,1)}), bf16[16,24,2048]{2,1,0:T(8,128)(2,1)}, u32[]{:S(2)}, u32[]{:S(2)}) async-start(bf16[16,24,2048]{2,1,0:T(8,128)(2,1)} %bitcast.50), calls=%async_computation.1 | async-start | bytes 3145728 | tf_op jit(solution)/shard_map/all_to_all | solution.py:45
  128.2 7.0 %copy-start.3 = (bf16[2048,16]{0,1:T(8,128)(2,1)S(1)}, bf16[2048,16]{0,1:T(8,128)(2,1)}, u32[]{:S(2)}) copy-start(bf16[2048,16]{0,1:T(8,128)(2,1)} %param.9) | copy-start | bytes 196612
  128.2 61.1 %all-to-all-start.3 = ((bf16[16,64,2048]{2,1,0:T(8,128)(2,1)}), bf16[16,64,2048]{2,1,0:T(8,128)(2,1)}, u32[]{:S(2)}, u32[]{:S(2)}) async-start(bf16[16,64,2048]{2,1,0:T(8,128)(2,1)} %bitcast.49), calls=%async_computation.3 | async-start | bytes 8388608 | tf_op jit(solution)/shard_map/all_to_all | solution.py:60
  135.4 2.5 %copy-start.4 = (s32[2]{0:T(128)S(1)}, s32[2]{0:T(128)}, u32[]{:S(2)}) copy-start(s32[2]{0:T(128)} %param.15) | copy-start | bytes 28
where the time goes:
time: 197 us; the launch traced here: 196 us
  waiting for transfers between devices  110 us (56%)
  matrix products  35.3 us (18%)
  starting transfers between devices  22.4 us (11%)
  local copies, waits for them, and re-layouts  15.1 us (8%)
  other arithmetic  12.8 us (6%)
    all_to_all x1, waiting for transfers between devices, shards(): lax.all_to_all(outgoing, 'expert', split_axis=0, concat_axis=0, tiled=True)  47.7 us
    all_to_all x2, waiting for transfers between devices, shards(): lax.all_to_all(answer, 'expert', split_axis=0, concat_axis=0, tiled=True)  40.2 us
    all_to_all x1, waiting for transfers between devices, shards(): lax.all_to_all(outbound, 'expert', split_axis=0, concat_axis=0, tiled=True)  22.2 us
    dot_general x2, matrix products, expert_swiglu(): jnp.dot(hidden, down_mat, preferred_element_type=jnp.float32)  19.2 us
    all_to_all x2, starting transfers between devices, shards(): lax.all_to_all(answer, 'expert', split_axis=0, concat_axis=0, tiled=True)  10.8 us
    dot_general x1, matrix products, expert_swiglu(): up_part = jnp.dot(inputs, up_mat, preferred_element_type=jnp.float32)  8.33 us
    gather x2, local copies, waits for them, and re-layouts, shards(): jnp.take(returned_flat, safe_cell, axis=0)  7.28 us
    all_to_all x1, starting transfers between devices, shards(): lax.all_to_all(outbound, 'expert', split_axis=0, concat_axis=0, tiled=True)  7.07 us
  transfers between devices with their start and end apart: 4, of which 4 were waited for; matrix products, arithmetic and copies ran while one was open for 26% of the time, Pallas kernels for 0%

commit v1 on v0

v1 whole, which is shorter than its diff:
```python
import functools

import jax
import jax.numpy as jnp
from jax import lax
from jax.experimental import pallas as pl
from jax.experimental.pallas import tpu as pltpu
from jax.sharding import PartitionSpec as P

MESH = pl.DeviceIdType.MESH
SIDE = 4
LO, HI = pl.ds(0, 16), pl.ds(16, 16)
N_SEMS = 128
FAR = 4096.0


def kernel(
    tokens, router, gate, up, down, routing, priority, hot_list, out,
    grid_tok, part, relay, final, summed, relay2, final2, shares, columns,
    w_gate, w_up, w_down, w_router, own, hidden, result, route_v, prio_v, hot_s,
    send_sem, recv_sem, local_sem,
):
    me = lax.axis_index("expert")
    my_y, my_x = me // SIDE, me % SIDE
    x_plus = my_y * SIDE + (my_x + 1) % SIDE
    x_minus = my_y * SIDE + (my_x + SIDE - 1) % SIDE
    y_plus = ((my_y + 1) % SIDE) * SIDE + my_x
    y_minus = ((my_y + SIDE - 1) % SIDE) * SIDE + my_x
    first = ((x_plus, x_minus), (y_plus, y_minus))
    second = ((y_plus, y_minus), (x_plus, x_minus))
    half = own.shape[1]
    n_ff = w_gate.shape[1]
    width = w_gate.shape[0]
    n_exp = SIDE * SIDE
    capacity = min(2 * half, 3 * prio_v.shape[1] // (2 * n_exp))

    copies = []

    def remote(src, dst, device):
        index = len(copies)
        made = pltpu.make_async_remote_copy(
            src_ref=src, dst_ref=dst, send_sem=send_sem.at[index], recv_sem=recv_sem.at[index],
            device_id={"expert": device}, device_id_type=MESH,
        )
        copies.append(made)
        made.start()
        return made

    local_count = [0]

    def local(src, dst):
        made = pltpu.make_async_copy(src, dst, local_sem.at[local_count[0]])
        local_count[0] += 1
        made.start()
        return made

    barrier = pltpu.get_barrier_semaphore()
    for device in (x_plus, x_minus, y_plus, y_minus):
        pl.semaphore_signal(barrier, inc=1, device_id={"expert": device}, device_id_type=MESH)
    own_in = [local(tokens.at[pl.ds(s * half, half)], own.at[s]) for s in range(2)]
    route_in = local(routing, route_v)
    prio_in = local(priority, prio_v)
    hot_in = local(hot_list, hot_s)
    router_in = local(router, w_router)
    slot_in = [
        local(tokens.at[pl.ds(s * half, half)], grid_tok.at[0, s, 0]) for s in range(2)
    ]
    pl.semaphore_wait(barrier, 4)

    ag1 = [None, None]
    ag2 = [[None] * SIDE, [None] * SIDE]
    ag2f = [[None] * SIDE, [None] * SIDE]
    for s in range(2):
        mine = tokens.at[pl.ds(s * half, half)]
        ag1[s] = (
            remote(mine, grid_tok.at[3, s, 0], first[s][0]),
            remote(mine, grid_tok.at[1, s, 0], first[s][1]),
        )
    for s in range(2):
        mine = tokens.at[pl.ds(s * half, half)]
        ag2[s][0] = (
            remote(mine, grid_tok.at[0, s, 3], second[s][0]),
            remote(mine, grid_tok.at[0, s, 1], second[s][1]),
        )
    gate_in = local(gate.at[0], w_gate)
    up_in = local(up.at[0], w_up)
    down_in = local(down.at[0], w_down)

    for made in own_in:
        made.wait()
    route_in.wait()
    prio_in.wait()
    hot_in.wait()
    router_in.wait()
    toks = 2 * half
    logits = jnp.concatenate(
        [jnp.dot(own[s], w_router[...], preferred_element_type=jnp.float32) for s in range(2)], axis=0
    )
    logits = jnp.concatenate(
        [logits, jnp.zeros((toks, 128 - n_exp), jnp.float32)], axis=1
    )
    sigmas = jax.nn.sigmoid(logits)
    lanes = lax.broadcasted_iota(jnp.int32, (toks, 128), 1)
    slot_at = lax.broadcasted_iota(jnp.int32, (toks, prio_v.shape[1]), 1)
    slot_of = lax.broadcasted_iota(jnp.int32, (toks, prio_v.shape[1]), 0) * SIDE
    order = jnp.broadcast_to(prio_v[...].astype(jnp.float32), (toks, prio_v.shape[1]))
    prior = jnp.full((toks, 128), FAR, jnp.float32)
    picked = jnp.zeros((toks, 128), jnp.float32)
    for k in range(route_v.shape[1]):
        hit = route_v[:, k : k + 1] == lanes
        place = jnp.sum(jnp.where(slot_at == slot_of + k, order, 0.0), axis=1, keepdims=True)
        prior = jnp.where(hit, place, prior)
        picked = jnp.where(hit, sigmas, picked)
    weights = picked / jnp.sum(picked, axis=1, keepdims=True)
    fill = jnp.full((128 - toks, 128), FAR, jnp.float32)
    prior_t = jnp.transpose(jnp.concatenate([prior, fill], axis=0))[:n_exp]
    weight_t = jnp.transpose(jnp.concatenate([weights, fill], axis=0))[:n_exp]
    experts = lax.broadcasted_iota(jnp.int32, (n_exp, 128), 0)
    rank_rows = []
    for e in range(n_exp):
        before = prior[:, e : e + 1] < prior_t[e : e + 1, :]
        rank_rows.append(jnp.sum(jnp.where(before, 1.0, 0.0), axis=0, keepdims=True))
    ranks = jnp.concatenate(rank_rows, axis=0)
    hot = (experts == hot_s[0]) | (experts == hot_s[1])
    token_at = lax.broadcasted_iota(jnp.int32, (n_exp, 128), 1)
    keep = (hot | (ranks < capacity)) & (token_at < toks)
    kept = jnp.where(keep, weight_t, 0.0)
    shares[0, 0] = kept[:8] + pltpu.roll(kept[8:], 64, axis=1)

    def forward_first(s):
        ag1[s][0].wait_recv()
        plus = remote(grid_tok.at[3, s, 0, LO], grid_tok.at[2, s, 0, LO], first[s][0])
        ag1[s][1].wait_recv()
        minus = remote(grid_tok.at[1, s, 0, HI], grid_tok.at[2, s, 0, HI], first[s][1])
        return plus, minus

    def spread(s, d):
        ag2[s][d] = (
            remote(grid_tok.at[d, s, 0], grid_tok.at[d, s, 3], second[s][0]),
            remote(grid_tok.at[d, s, 0], grid_tok.at[d, s, 1], second[s][1]),
        )

    def forward_second(s, d):
        ag2[s][d][0].wait_recv()
        plus = remote(grid_tok.at[d, s, 3, LO], grid_tok.at[d, s, 2, LO], second[s][0])
        ag2[s][d][1].wait_recv()
        minus = remote(grid_tok.at[d, s, 1, HI], grid_tok.at[d, s, 2, HI], second[s][1])
        ag2f[s][d] = (plus, minus)

    share_x = (
        remote(shares.at[0, 0], shares.at[3, 0], x_plus),
        remote(shares.at[0, 0], shares.at[1, 0], x_minus),
    )
    ag1f = [forward_first(s) for s in range(2)]
    for s in range(2):
        spread(s, 3)
    for s in range(2):
        spread(s, 1)
    share_x[0].wait_recv()
    share_x2 = remote(shares.at[3, 0], shares.at[2, 0], x_plus)
    for s in range(2):
        forward_second(s, 0)
    for s in range(2):
        ag1f[s][0].wait_recv()
        ag1f[s][1].wait_recv()
        spread(s, 2)
    share_x[1].wait_recv()
    share_x2.wait_recv()
    share_y = (
        remote(shares.at[:, 0], shares.at[:, 3], y_plus),
        remote(shares.at[:, 0], shares.at[:, 1], y_minus),
    )
    for s in range(2):
        forward_second(s, 3)
    share_y[0].wait_recv()
    share_y2 = remote(shares.at[:, 3], shares.at[:, 2], y_plus)
    for s in range(2):
        slot_in[s].wait()
    gate_in.wait()
    up_in.wait()
    down_in.wait()
    share_y[1].wait_recv()
    share_y2.wait_recv()

    my_row, my_half = me % 8, me // 8
    share_row = lax.broadcasted_iota(jnp.int32, (8, 128), 0) == my_row
    token_lane = lax.broadcasted_iota(jnp.int32, (half, 128), 1)
    token_row = lax.broadcasted_iota(jnp.int32, (half, 128), 0)

    def expert(d):
        for s in range(2):
            pick = token_lane == token_row + (my_half * 64 + s * half)
            for e in range(SIDE):
                held = shares[d, e] if s == 0 else shares[e, d]
                row = jnp.sum(jnp.where(share_row, held, 0.0), axis=0, keepdims=True)
                row = jnp.broadcast_to(row, (half, 128))
                columns[pl.ds((s * SIDE + e) * half, half)] = jnp.broadcast_to(
                    jnp.sum(jnp.where(pick, row, 0.0), axis=1, keepdims=True), (half, 128)
                )
        rows = 2 * SIDE * half

        def inner(n, carry):
            at = pl.ds(pl.multiple_of(n * 256, 256), 256)
            block = grid_tok[d].reshape(rows, width)
            g = jnp.dot(block, w_gate[:, at], preferred_element_type=jnp.float32)
            u = jnp.dot(block, w_up[:, at], preferred_element_type=jnp.float32)
            hidden[:, at] = (g / (1.0 + jnp.exp(-g)) * u).astype(jnp.bfloat16)
            return carry

        lax.fori_loop(0, n_ff // 256, inner, 0)

        def outer(n, carry):
            at = pl.ds(pl.multiple_of(n * 256, 256), 256)
            o = jnp.dot(hidden[...], w_down[:, at], preferred_element_type=jnp.float32)
            scale = jnp.concatenate([columns[...], columns[...]], axis=1)
            part[d, :, :, :, at] = (o * scale).astype(jnp.bfloat16).reshape(2, SIDE, half, 256)
            return carry

        lax.fori_loop(0, width // 256, outer, 0)

    rs1f = [[None] * SIDE, [None] * SIDE]
    rs1 = [[None] * SIDE, [None] * SIDE]

    def reduce_start(s, d):
        rs1f[s][d] = (
            remote(part.at[d, s, 2, LO], relay.at[d, s, 0], second[s][0]),
            remote(part.at[d, s, 2, HI], relay.at[d, s, 1], second[s][1]),
        )
        rs1[s][d] = [
            remote(part.at[d, s, 1, HI], final.at[d, s, 0, HI], second[s][0]),
            remote(part.at[d, s, 3, LO], final.at[d, s, 1, LO], second[s][1]),
        ]

    def total(*values):
        result = values[0].astype(jnp.float32)
        for value in values[1:]:
            result = result + value.astype(jnp.float32)
        return result

    def reduce_relay(s, d):
        rs1f[s][d][0].wait_recv()
        part[d, s, 1, LO] = total(part[d, s, 1, LO], relay[d, s, 0]).astype(jnp.bfloat16)
        rs1f[s][d][1].wait_recv()
        part[d, s, 3, HI] = total(part[d, s, 3, HI], relay[d, s, 1]).astype(jnp.bfloat16)
        rs1[s][d] += [
            remote(part.at[d, s, 1, LO], final.at[d, s, 0, LO], second[s][0]),
            remote(part.at[d, s, 3, HI], final.at[d, s, 1, HI], second[s][1]),
        ]

    def reduce_finish(s, d):
        for made in rs1[s][d]:
            made.wait_recv()
        summed[d, s] = total(part[d, s, 0], final[d, s, 0], final[d, s, 1]).astype(jnp.bfloat16)

    for s in range(2):
        ag2f[s][0][0].wait_recv()
        ag2f[s][0][1].wait_recv()
    expert(0)
    for s in range(2):
        reduce_start(s, 0)
    for s in range(2):
        forward_second(s, 1)
    for s in range(2):
        forward_second(s, 2)
    for s in range(2):
        ag2f[s][3][0].wait_recv()
        ag2f[s][3][1].wait_recv()
    expert(3)
    for s in range(2):
        reduce_start(s, 3)
    for s in range(2):
        reduce_relay(s, 0)
    for s in range(2):
        ag2f[s][1][0].wait_recv()
        ag2f[s][1][1].wait_recv()
    expert(1)
    for s in range(2):
        reduce_start(s, 1)
    for s in range(2):
        reduce_relay(s, 3)
    for s in range(2):
        ag2f[s][2][0].wait_recv()
        ag2f[s][2][1].wait_recv()
    expert(2)
    for s in range(2):
        reduce_start(s, 2)
    for s in range(2):
        reduce_relay(s, 1)
    for s in range(2):
        reduce_relay(s, 2)
    rs2 = [None, None]
    rs2f = [None, None]
    for d in (0, 3, 1):
        for s in range(2):
            reduce_finish(s, d)
    for s in range(2):
        rs2[s] = [
            remote(summed.at[1, s, HI], final2.at[s, 0, HI], first[s][0]),
            remote(summed.at[3, s, LO], final2.at[s, 1, LO], first[s][1]),
        ]
    for s in range(2):
        reduce_finish(s, 2)
    for s in range(2):
        rs2f[s] = (
            remote(summed.at[2, s, LO], relay2.at[s, 0], first[s][0]),
            remote(summed.at[2, s, HI], relay2.at[s, 1], first[s][1]),
        )
    for s in range(2):
        rs2f[s][0].wait_recv()
        summed[1, s, LO] = total(summed[1, s, LO], relay2[s, 0]).astype(jnp.bfloat16)
        rs2f[s][1].wait_recv()
        summed[3, s, HI] = total(summed[3, s, HI], relay2[s, 1]).astype(jnp.bfloat16)
        rs2[s] += [
            remote(summed.at[1, s, LO], final2.at[s, 0, LO], first[s][0]),
            remote(summed.at[3, s, HI], final2.at[s, 1, HI], first[s][1]),
        ]
    for s in range(2):
        for made in rs2[s]:
            made.wait_recv()
        result[pl.ds(s * half, half)] = total(
            summed[0, s], final2[s, 0], final2[s, 1]
        ).astype(jnp.bfloat16)
    out_copy = local(result, out)
    for made in copies:
        made.wait_send()
    out_copy.wait()


def shards(tokens, router_weight, gate_weight, up_weight, down_weight, routing, priority, hot_list):
    toks, width = tokens.shape
    half = toks // 2
    n_ff = gate_weight.shape[2]
    bf16, f32 = jnp.bfloat16, jnp.float32
    any_spec = pl.BlockSpec(memory_space=pl.ANY)
    return pl.pallas_call(
        kernel,
        out_shape=jax.ShapeDtypeStruct((toks, width), bf16),
        in_specs=[any_spec] * 8,
        out_specs=any_spec,
        scratch_shapes=[
            pltpu.VMEM((SIDE, 2, SIDE, half, width), bf16),
            pltpu.VMEM((SIDE, 2, SIDE, half, width), bf16),
            pltpu.VMEM((SIDE, 2, 2, half // 2, width), bf16),
            pltpu.VMEM((SIDE, 2, 2, half, width), bf16),
            pltpu.VMEM((SIDE, 2, half, width), bf16),
            pltpu.VMEM((2, 2, half // 2, width), bf16),
            pltpu.VMEM((2, 2, half, width), bf16),
            pltpu.VMEM((SIDE, SIDE, 8, 128), f32),
            pltpu.VMEM((2 * SIDE * half, 128), f32),
            pltpu.VMEM((width, n_ff), bf16),
            pltpu.VMEM((width, n_ff), bf16),
            pltpu.VMEM((n_ff, width), bf16),
            pltpu.VMEM(router_weight.shape, bf16),
            pltpu.VMEM((2, half, width), bf16),
            pltpu.VMEM((2 * SIDE * half, n_ff), bf16),
            pltpu.VMEM((toks, width), bf16),
            pltpu.VMEM(routing.shape, jnp.int32),
            pltpu.VMEM(priority.shape, jnp.int32),
            pltpu.SMEM(hot_list.shape, jnp.int32),
            pltpu.SemaphoreType.DMA((N_SEMS,)),
            pltpu.SemaphoreType.DMA((N_SEMS,)),
            pltpu.SemaphoreType.DMA((16,)),
        ],
        compiler_params=pltpu.CompilerParams(
            collective_id=0, has_side_effects=True, vmem_limit_bytes=48 * 1024 * 1024
        ),
    )(tokens, router_weight, gate_weight, up_weight, down_weight, routing, priority, hot_list)


def solution(mesh):
    return jax.shard_map(
        shards,
        mesh=mesh,
        in_specs=(
            P(("dp", "expert"), None),
            P(),
            P("expert", None, None),
            P("expert", None, None),
            P("expert", None, None),
            P(("dp", "expert"), None),
            P(("dp", "expert"), None),
            P("dp"),
        ),
        out_specs=P(("dp", "expert"), None),
        check_vma=False,
    )
```

time: 197 us -> 72.4 us (0.37)
  waiting for transfers between devices: 110 us -> 0 us
  Pallas kernels: 0 us -> 65.4 us
  matrix products: 35.3 us -> 0 us
  starting transfers between devices: 22.4 us -> 0 us
  other arithmetic: 12.8 us -> 0 us
  local copies, waits for them, and re-layouts: 15.1 us -> 6.75 us
    all_to_all x4 -> x0, waiting for transfers between devices: 110 us -> none  [the longest x1 47.7 us: shards(): lax.all_to_all(outgoing, 'expert', split_axis=0, concat_axis=0, tiled=True)]
    pallas_call x0 -> x1, Pallas kernels: none -> 65.4 us  [shards(): pl.pallas_call(kernel, out_shape=jax.ShapeDtypeStruct((toks, width), bf16...]
    dot_general x6 -> x0, matrix products: 35.3 us -> none  [the longest x2 19.2 us: expert_swiglu(): jnp.dot(hidden, down_mat, preferred_element_type=jnp.float32)]
    all_to_all x4 -> x0, starting transfers between devices: 22.4 us -> none  [the longest x2 10.8 us: shards(): lax.all_to_all(answer, 'expert', split_axis=0, concat_axis=0, tiled=True)]
    gather x8 -> x0, local copies, waits for them, and re-layouts: 13.2 us -> none  [the longest x2 7.28 us: shards(): jnp.take(returned_flat, safe_cell, axis=0)]
    reduce_sum x6 -> x0, other arithmetic: 7.17 us -> none  [the longest x1 4.67 us: shards(): jnp.sum(slot_weight[:, :, None] * slot_answer.astype(jnp.float32), axis=1)]
    unnamed x11, local copies, waits for them, and re-layouts: 0.94 us -> 6.75 us
    select_n x4 -> x0, other arithmetic: 2.35 us -> none  [the longest x1 2.31 us: shards(): jnp.where(asked[:, :, None], tokens[None, :, :], jnp.zeros((), jnp.bfloat...]
  transfers between devices with their start and end apart: 4 -> 0, of which waited for: 4 -> 0; matrix products, arithmetic and copies ran while one was open for 26% -> 0% of each run, Pallas kernels for 0% -> 0%
where the time goes in v1:
time: 72.4 us; the launch traced here: 72.2 us
  Pallas kernels  65.4 us (90%)
  local copies, waits for them, and re-layouts  6.75 us (9%)
    pallas_call x1, Pallas kernels, shards(): pl.pallas_call(kernel, out_shape=jax.ShapeDtypeStruct((toks, width), bf16...  65.4 us
    unnamed x11, local copies, waits for them, and re-layouts  6.75 us

profile of v1, /device:TPU:32, one launch (start us, length us, event | category | flops | bytes accessed | tf_op | source)
XLA Modules:
  0.0 72.2 jit_solution(7344791198877058570)
XLA Ops:
  0.0 0.8 %copy.10.routing = s32[64,4]{1,0:T(8,128)S(1)} copy(s32[64,4]{0,1:T(4,128)} %param.13) | data formatting | bytes 2048 | tf_op args[5]
  0.8 1.1 %copy.9.router = bf16[2048,16]{1,0:T(8,128)(2,1)S(1)} copy(bf16[2048,16]{0,1:T(8,128)(2,1)} %param.9) | data formatting | bytes 131072 | tf_op args[1]
  1.9 0.0 copy-start
  1.9 1.9 %copy-done = bf16[1,2048,768]{2,1,0:T(8,128)(2,1)S(1)} copy-done((bf16[1,2048,768]{2,1,0:T(8,128)(2,1)S(1)}, bf16[1,2048,768]{2,1,0:T(8,128)(2,1)}, u32[]{:S(2)}) %copy-start) | copy-done | bytes 3145752
  3.8 0.0 copy-start.1
  3.8 0.9 %copy-done.1 = bf16[64,2048]{1,0:T(8,128)(2,1)S(1)} copy-done((bf16[64,2048]{1,0:T(8,128)(2,1)S(1)}, bf16[64,2048]{1,0:T(8,128)(2,1)}, u32[]{:S(2)}) %copy-start.1) | copy-done | bytes 262168
  4.7 0.0 copy-start.2
  4.7 0.7 copy-done.2
  5.4 0.0 copy-start.3
  5.4 0.7 copy-done.3
  6.1 65.4 %shard_map.82 = bf16[64,2048]{1,0:T(8,128)(2,1)S(1)} custom-call(bf16[64,2048]{1,0:T(8,128)(2,1)S(1)} %copy-done.1, bf16[2048,16]{1,0:T(8,128)(2,1)S(1)} %copy.9.router, bf16[1,2048,768]{2,1,0:T(8,128)(2,1)S(1)} %copy-done, bf16[1,2048,768]{2,1,0:T(8,128)(2,1)} %up.1, bf16[1,768,2048]{2,1,0:T(8,128)(2,1)} %down.1, s32[64,4]{1,0:T(8,128)S(1)} %copy.10.routing, ...), custom_call_target="tpu_custom_call" | custom-call | tf_op jit(solution)/shard_map/pallas_call | solution.py:335
  71.5 0.7 copy.12
Async XLA Ops:
  1.9 1.9 %copy-start = (bf16[1,2048,768]{2,1,0:T(8,128)(2,1)S(1)}, bf16[1,2048,768]{2,1,0:T(8,128)(2,1)}, u32[]{:S(2)}) copy-start(bf16[1,2048,768]{2,1,0:T(8,128)(2,1)} %gate.1) | copy-start | bytes 9437188
  3.8 0.9 %copy-start.1 = (bf16[64,2048]{1,0:T(8,128)(2,1)S(1)}, bf16[64,2048]{1,0:T(8,128)(2,1)}, u32[]{:S(2)}) copy-start(bf16[64,2048]{1,0:T(8,128)(2,1)} %tokens.1) | copy-start | bytes 786436
  4.7 0.7 copy-start.2
  5.4 0.7 copy-start.3

commit v2 on v0

v2 whole, which is shorter than its diff:
```python
import jax
import jax.numpy as jnp
from jax import lax
from jax.experimental import pallas as pl
from jax.experimental.pallas import tpu as pltpu
from jax.sharding import PartitionSpec as P

MESH = pl.DeviceIdType.MESH
SIDE = 4
LO, HI = pl.ds(0, 16), pl.ds(16, 16)
N_SEMS = 128
FAR = 4096.0
ORDER = (
    ("O", 1), ("O", 0), ("S", 0, 0), ("S", 0, 1), ("X",), ("f", 0, 1), ("f", 0, 0), ("f", 1, 0),
    ("f", 1, 1), ("S", 3, 0), ("S", 3, 1), ("g", 1, 0, 0), ("g", 0, 0, 0), ("g", 0, 0, 1),
    ("g", 1, 0, 1), ("Y",), ("S", 2, 1), ("S", 2, 0), ("g", 0, 3, 1), ("g", 1, 3, 1), ("g", 0, 3, 0),
    ("g", 1, 3, 0), ("S", 1, 1), ("S", 1, 0), ("E", 0, 0), ("E", 0, 1), ("g", 1, 2, 1), ("g", 1, 2, 0),
    ("g", 0, 2, 1), ("g", 0, 2, 0), ("E", 3, 1), ("b", 0, 1), ("b", 0, 0), ("E", 3, 0), ("b", 3, 1),
    ("a", 3, 0), ("g", 0, 1, 1), ("g", 1, 1, 1), ("g", 0, 1, 0), ("g", 1, 1, 0), ("E", 2, 1),
    ("b", 2, 1), ("E", 2, 0), ("b", 2, 0), ("a", 2, 0), ("a", 2, 1), ("r", 0, 3, 0), ("a", 3, 1),
    ("r", 1, 3, 0), ("E", 1, 1), ("a", 1, 1), ("E", 1, 0), ("a", 1, 0), ("b", 3, 0), ("r", 0, 2, 1),
    ("r", 1, 2, 1), ("b", 1, 1), ("r", 0, 2, 0), ("r", 1, 2, 0), ("r", 0, 3, 1), ("r", 1, 3, 1),
    ("b", 1, 0), ("r", 0, 1, 1), ("r", 1, 1, 1), ("r", 0, 1, 0), ("r", 1, 1, 0), ("F", 2, 1), ("A", 1),
    ("F", 3, 0), ("a", 0, 1), ("F", 2, 0), ("A", 0), ("a", 0, 0), ("F", 3, 1), ("B", 0, 0), ("B", 0, 1),
    ("F", 1, 1), ("B", 1, 1), ("F", 1, 0), ("B", 1, 0), ("r", 0, 0, 1), ("r", 1, 0, 1), ("R", 0, 1),
    ("R", 1, 1), ("R", 0, 0), ("R", 1, 0), ("r", 0, 0, 0), ("r", 1, 0, 0), ("Z", 1), ("Z", 0),
)


def kernel(
    tokens, router, gate, up, down, routing, priority, hot_list, out,
    grid_tok, part, relay, final, summed, relay2, final2, shares, columns,
    w_gate, w_up, w_down, w_router, own, hidden, result, route_v, prio_v, hot_s,
    send_sem, recv_sem, local_sem, far_sem,
):
    me = lax.axis_index("expert")
    my_y, my_x = me // SIDE, me % SIDE
    x_plus = my_y * SIDE + (my_x + 1) % SIDE
    x_minus = my_y * SIDE + (my_x + SIDE - 1) % SIDE
    y_plus = ((my_y + 1) % SIDE) * SIDE + my_x
    y_minus = ((my_y + SIDE - 1) % SIDE) * SIDE + my_x
    x_far = my_y * SIDE + (my_x + 2) % SIDE
    y_far = ((my_y + 2) % SIDE) * SIDE + my_x
    first = ((x_plus, x_minus), (y_plus, y_minus))
    second = ((y_plus, y_minus), (x_plus, x_minus))
    half = own.shape[1]
    n_ff = w_gate.shape[1]
    width = w_gate.shape[0]
    n_exp = SIDE * SIDE
    capacity = min(2 * half, 3 * prio_v.shape[1] // (2 * n_exp))

    copies, landed = {}, set()

    def remote(key, src, dst, device):
        index = len(copies)
        copies[key] = pltpu.make_async_remote_copy(
            src_ref=src, dst_ref=dst, send_sem=send_sem.at[index], recv_sem=recv_sem.at[index],
            device_id={"expert": device}, device_id_type=MESH,
        )
        copies[key].start()

    def got(*keys):
        for key in keys:
            if key not in landed:
                landed.add(key)
                copies[key].wait_recv()

    local_count = [0]

    def local(src, dst):
        made = pltpu.make_async_copy(src, dst, local_sem.at[local_count[0]])
        local_count[0] += 1
        made.start()
        return made

    barrier = pltpu.get_barrier_semaphore()
    for device in (x_plus, x_minus, y_plus, y_minus):
        pl.semaphore_signal(barrier, inc=1, device_id={"expert": device}, device_id_type=MESH)
    own_in = [local(tokens.at[pl.ds(s * half, half)], own.at[s]) for s in range(2)]
    small_in = [
        local(routing, route_v), local(priority, prio_v), local(hot_list, hot_s), local(router, w_router)
    ]
    pl.semaphore_wait(barrier, 4)

    def own_first(s):
        mine = tokens.at[pl.ds(s * half, half)]
        remote(("O+", s), mine, grid_tok.at[3, s, 0], first[s][0])
        remote(("O-", s), mine, grid_tok.at[1, s, 0], first[s][1])

    def spread(d, s):
        if d == 0:
            mine = tokens.at[pl.ds(s * half, half)]
        else:
            got(*{3: [("O+", s)], 1: [("O-", s)], 2: [("f+", s), ("f-", s)]}[d])
            mine = grid_tok.at[d, s, 0]
        remote(("S+", d, s), mine, grid_tok.at[d, s, 3], second[s][0])
        remote(("S-", d, s), mine, grid_tok.at[d, s, 1], second[s][1])

    def pass_first(plus, s):
        if plus:
            got(("O+", s))
            remote(("f+", s), grid_tok.at[3, s, 0, LO], grid_tok.at[2, s, 0, LO], first[s][0])
        else:
            got(("O-", s))
            remote(("f-", s), grid_tok.at[1, s, 0, HI], grid_tok.at[2, s, 0, HI], first[s][1])

    def pass_second(plus, d, s):
        if plus:
            got(("S+", d, s))
            remote(("g+", d, s), grid_tok.at[d, s, 3, LO], grid_tok.at[d, s, 2, LO], second[s][0])
        else:
            got(("S-", d, s))
            remote(("g-", d, s), grid_tok.at[d, s, 1, HI], grid_tok.at[d, s, 2, HI], second[s][1])

    def share_x():
        make_shares()
        pl.semaphore_wait(far_sem.at[0], 1)
        remote("X+", shares.at[0, 0], shares.at[3, 0], x_plus)
        remote("X-", shares.at[0, 0], shares.at[1, 0], x_minus)
        remote("X2", shares.at[0, 0], shares.at[2, 0], x_far)

    def share_y():
        got("X+", "X-", "X2")
        pl.semaphore_wait(far_sem.at[1], 1)
        remote("Y+", shares.at[:, 0], shares.at[:, 3], y_plus)
        remote("Y-", shares.at[:, 0], shares.at[:, 1], y_minus)
        remote("Y2", shares.at[:, 0], shares.at[:, 2], y_far)

    my_row, my_half = me % 8, me // 8
    rows = SIDE * half
    loaded = []

    def expert(d, s):
        if not loaded:
            got("X+", "X-", "X2", "Y+", "Y-", "Y2")
            for made in heavy_in:
                made.wait()
            loaded.append(1)
        got(("S+", d, s), ("S-", d, s), ("g+", d, s), ("g-", d, s))
        got(*{0: [], 3: [("O+", s)], 1: [("O-", s)], 2: [("f+", s), ("f-", s)]}[d])
        share_row = lax.broadcasted_iota(jnp.int32, (8, 128), 0) == my_row
        token_lane = lax.broadcasted_iota(jnp.int32, (half, 128), 1)
        token_row = lax.broadcasted_iota(jnp.int32, (half, 128), 0)
        pick = token_lane == token_row + (my_half * 64 + s * half)
        for e in range(SIDE):
            held = shares[d, e] if s == 0 else shares[e, d]
            row = jnp.sum(jnp.where(share_row, held, 0.0), axis=0, keepdims=True)
            row = jnp.broadcast_to(row, (half, 128))
            columns[pl.ds(e * half, half)] = jnp.broadcast_to(
                jnp.sum(jnp.where(pick, row, 0.0), axis=1, keepdims=True), (half, 128)
            )
        for n in range(n_ff // 256):
            at = pl.ds(n * 256, 256)
            block = grid_tok[d, s].reshape(rows, width)
            g = jnp.dot(block, w_gate[:, at], preferred_element_type=jnp.float32)
            u = jnp.dot(block, w_up[:, at], preferred_element_type=jnp.float32)
            hidden[:, at] = (g / (1.0 + jnp.exp(-g)) * u).astype(jnp.bfloat16)
        for n in range(width // 256):
            at = pl.ds(n * 256, 256)
            o = jnp.dot(hidden[...], w_down[:, at], preferred_element_type=jnp.float32)
            scale = jnp.concatenate([columns[...], columns[...]], axis=1)
            part[d, s, :, :, at] = (o * scale).astype(jnp.bfloat16).reshape(SIDE, half, 256)

    def total(*values):
        result = values[0].astype(jnp.float32)
        for value in values[1:]:
            result = result + value.astype(jnp.float32)
        return result

    def far_halves(d, s):
        remote(("a+", d, s), part.at[d, s, 2, LO], relay.at[d, s, 0], second[s][0])
        remote(("a-", d, s), part.at[d, s, 2, HI], relay.at[d, s, 1], second[s][1])

    def near_halves(d, s):
        remote(("b+", d, s), part.at[d, s, 1, HI], final.at[d, s, 0, HI], second[s][0])
        remote(("b-", d, s), part.at[d, s, 3, LO], final.at[d, s, 1, LO], second[s][1])

    def add_second(plus, d, s):
        if plus:
            got(("a+", d, s))
            part[d, s, 1, LO] = total(part[d, s, 1, LO], relay[d, s, 0]).astype(jnp.bfloat16)
            remote(("r+", d, s), part.at[d, s, 1, LO], final.at[d, s, 0, LO], second[s][0])
        else:
            got(("a-", d, s))
            part[d, s, 3, HI] = total(part[d, s, 3, HI], relay[d, s, 1]).astype(jnp.bfloat16)
            remote(("r-", d, s), part.at[d, s, 3, HI], final.at[d, s, 1, HI], second[s][1])

    def fold(d, s):
        got(("b+", d, s), ("b-", d, s), ("r+", d, s), ("r-", d, s))
        summed[d, s] = total(part[d, s, 0], final[d, s, 0], final[d, s, 1]).astype(jnp.bfloat16)

    def far_first(s):
        remote(("A+", s), summed.at[2, s, LO], relay2.at[s, 0], first[s][0])
        remote(("A-", s), summed.at[2, s, HI], relay2.at[s, 1], first[s][1])

    def near_first(plus, s):
        if plus:
            remote(("B+", s), summed.at[1, s, HI], final2.at[s, 0, HI], first[s][0])
        else:
            remote(("B-", s), summed.at[3, s, LO], final2.at[s, 1, LO], first[s][1])

    def add_first(plus, s):
        if plus:
            got(("A+", s))
            summed[1, s, LO] = total(summed[1, s, LO], relay2[s, 0]).astype(jnp.bfloat16)
            remote(("R+", s), summed.at[1, s, LO], final2.at[s, 0, LO], first[s][0])
        else:
            got(("A-", s))
            summed[3, s, HI] = total(summed[3, s, HI], relay2[s, 1]).astype(jnp.bfloat16)
            remote(("R-", s), summed.at[3, s, HI], final2.at[s, 1, HI], first[s][1])

    out_copies = []

    def finish(s):
        got(("b+", 0, s), ("b-", 0, s), ("r+", 0, s), ("r-", 0, s))
        got(("B+", s), ("B-", s), ("R+", s), ("R-", s))
        at = pl.ds(s * half, half)
        result[at] = total(
            part[0, s, 0], final[0, s, 0], final[0, s, 1], final2[s, 0], final2[s, 1]
        ).astype(jnp.bfloat16)
        out_copies.append(local(result.at[at], out.at[at]))

    def make_shares():
        for made in own_in + small_in:
            made.wait()
        toks = 2 * half
        contract = (((1,), (1,)), ((), ()))
        logits = jnp.concatenate(
            [
                lax.dot_general(w_router[...], own[s], contract, preferred_element_type=jnp.float32)
                for s in range(2)
            ]
            + [jnp.zeros((n_exp, 128 - toks), jnp.float32)],
            axis=1,
        )
        sigmas = jax.nn.sigmoid(logits)
        experts = lax.broadcasted_iota(jnp.int32, (n_exp, 128), 0)
        slots = prio_v.shape[1]
        slot_at = lax.broadcasted_iota(jnp.int32, (slots, 128), 0)
        slot_of = lax.broadcasted_iota(jnp.int32, (slots, 128), 1) * SIDE
        order = jnp.broadcast_to(prio_v[...].astype(jnp.float32), (8, slots)).astype(jnp.bfloat16)
        prior = jnp.full((n_exp, 128), FAR, jnp.float32)
        picked = jnp.zeros((n_exp, 128), jnp.float32)
        for k in range(route_v.shape[0]):
            chosen = jnp.concatenate(
                [route_v[k : k + 1, :], jnp.full((1, 128 - toks), -1, jnp.int32)], axis=1
            )
            hit = chosen == experts
            select = jnp.where(slot_at == slot_of + k, 1.0, 0.0).astype(jnp.bfloat16)
            place = jnp.dot(order, select, preferred_element_type=jnp.float32)[:1]
            prior = jnp.where(hit, place, prior)
            picked = jnp.where(hit, sigmas, picked)
        weights = picked / jnp.sum(picked, axis=0, keepdims=True)
        prior_t = jnp.transpose(
            jnp.concatenate([prior, jnp.full((128 - n_exp, 128), FAR, jnp.float32)], axis=0)
        )[:toks]
        rank_rows = []
        for e in range(n_exp):
            before = prior_t[:, e : e + 1] < prior[e : e + 1, :]
            rank_rows.append(jnp.sum(jnp.where(before, 1.0, 0.0), axis=0, keepdims=True))
        ranks = jnp.concatenate(rank_rows, axis=0)
        hot = (experts == hot_s[0]) | (experts == hot_s[1])
        token_at = lax.broadcasted_iota(jnp.int32, (n_exp, 128), 1)
        keep = (hot | (ranks < capacity)) & (token_at < toks)
        kept = jnp.where(keep, weights, 0.0)
        shares[0, 0] = kept[:8] + pltpu.roll(kept[8:], 64, axis=1)

    run = {
        "O": own_first, "S": spread, "f": pass_first, "g": pass_second, "X": share_x, "Y": share_y,
        "E": expert, "a": far_halves, "b": near_halves, "r": add_second, "F": fold, "A": far_first,
        "B": near_first, "R": add_first, "Z": finish,
    }
    heavy_in = []
    for at, step in enumerate(ORDER):
        if at == 4:
            pl.semaphore_signal(
                far_sem.at[0], inc=1, device_id={"expert": x_plus}, device_id_type=MESH
            )
            pl.semaphore_signal(
                far_sem.at[1], inc=1, device_id={"expert": y_plus}, device_id_type=MESH
            )
            heavy_in += [
                local(tokens.at[pl.ds(s * half, half)], grid_tok.at[0, s, 0]) for s in range(2)
            ]
            heavy_in += [
                local(gate.at[0], w_gate), local(up.at[0], w_up), local(down.at[0], w_down)
            ]
        run[step[0]](*step[1:])
    assert len(landed) == len(copies)
    for made in copies.values():
        made.wait_send()
    for made in out_copies:
        made.wait()


def shards(tokens, router_weight, gate_weight, up_weight, down_weight, routing, priority, hot_list):
    toks, width = tokens.shape
    half = toks // 2
    n_ff = gate_weight.shape[2]
    bf16, f32 = jnp.bfloat16, jnp.float32
    hbm = pl.BlockSpec(memory_space=pltpu.HBM)
    return pl.pallas_call(
        kernel,
        out_shape=jax.ShapeDtypeStruct((toks, width), bf16),
        in_specs=[hbm] * 8,
        out_specs=hbm,
        scratch_shapes=[
            pltpu.VMEM((SIDE, 2, SIDE, half, width), bf16),
            pltpu.VMEM((SIDE, 2, SIDE, half, width), bf16),
            pltpu.VMEM((SIDE, 2, 2, half // 2, width), bf16),
            pltpu.VMEM((SIDE, 2, 2, half, width), bf16),
            pltpu.VMEM((SIDE, 2, half, width), bf16),
            pltpu.VMEM((2, 2, half // 2, width), bf16),
            pltpu.VMEM((2, 2, half, width), bf16),
            pltpu.VMEM((SIDE, SIDE, 8, 128), f32),
            pltpu.VMEM((SIDE * half, 128), f32),
            pltpu.VMEM((width, n_ff), bf16),
            pltpu.VMEM((width, n_ff), bf16),
            pltpu.VMEM((n_ff, width), bf16),
            pltpu.VMEM(router_weight.shape[::-1], bf16),
            pltpu.VMEM((2, half, width), bf16),
            pltpu.VMEM((SIDE * half, n_ff), bf16),
            pltpu.VMEM((toks, width), bf16),
            pltpu.VMEM(routing.shape[::-1], jnp.int32),
            pltpu.VMEM(priority.shape, jnp.int32),
            pltpu.SMEM(hot_list.shape, jnp.int32),
            pltpu.SemaphoreType.DMA((N_SEMS,)),
            pltpu.SemaphoreType.DMA((N_SEMS,)),
            pltpu.SemaphoreType.DMA((16,)),
            pltpu.SemaphoreType.REGULAR((2,)),
        ],
        compiler_params=pltpu.CompilerParams(
            collective_id=0, has_side_effects=True, vmem_limit_bytes=67043328
        ),
    )(
        tokens, router_weight.T, gate_weight, up_weight, down_weight, routing.T, priority, hot_list
    )


def solution(mesh):
    return jax.shard_map(
        shards,
        mesh=mesh,
        in_specs=(
            P(("dp", "expert"), None),
            P(),
            P("expert", None, None),
            P("expert", None, None),
            P("expert", None, None),
            P(("dp", "expert"), None),
            P(("dp", "expert"), None),
            P("dp"),
        ),
        out_specs=P(("dp", "expert"), None),
        check_vma=False,
    )
```

time: 197 us -> 56.5 us (0.29)
  waiting for transfers between devices: 110 us -> 0 us
  Pallas kernels: 0 us -> 54.7 us
  matrix products: 35.3 us -> 0 us
  starting transfers between devices: 22.4 us -> 0 us
  local copies, waits for them, and re-layouts: 15.1 us -> 1.67 us
  other arithmetic: 12.8 us -> 0 us
    all_to_all x4 -> x0, waiting for transfers between devices: 110 us -> none  [the longest x1 47.7 us: shards(): lax.all_to_all(outgoing, 'expert', split_axis=0, concat_axis=0, tiled=True)]
    pallas_call x0 -> x1, Pallas kernels: none -> 54.7 us  [shards(): pl.pallas_call(kernel, out_shape=jax.ShapeDtypeStruct((toks, width), bf16...]
    dot_general x6 -> x0, matrix products: 35.3 us -> none  [the longest x2 19.2 us: expert_swiglu(): jnp.dot(hidden, down_mat, preferred_element_type=jnp.float32)]
    all_to_all x4 -> x0, starting transfers between devices: 22.4 us -> none  [the longest x2 10.8 us: shards(): lax.all_to_all(answer, 'expert', split_axis=0, concat_axis=0, tiled=True)]
    gather x8 -> x0, local copies, waits for them, and re-layouts: 13.2 us -> none  [the longest x2 7.28 us: shards(): jnp.take(returned_flat, safe_cell, axis=0)]
    reduce_sum x6 -> x0, other arithmetic: 7.17 us -> none  [the longest x1 4.67 us: shards(): jnp.sum(slot_weight[:, :, None] * slot_answer.astype(jnp.float32), axis=1)]
    select_n x4 -> x0, other arithmetic: 2.35 us -> none  [the longest x1 2.31 us: shards(): jnp.where(asked[:, :, None], tokens[None, :, :], jnp.zeros((), jnp.bfloat...]
  transfers between devices with their start and end apart: 4 -> 0, of which waited for: 4 -> 0; matrix products, arithmetic and copies ran while one was open for 26% -> 0% of each run, Pallas kernels for 0% -> 0%
where the time goes in v2:
time: 56.5 us; the launch traced here: 56.4 us
  Pallas kernels  54.7 us (97%)
  local copies, waits for them, and re-layouts  1.67 us (3%)
    pallas_call x1, Pallas kernels, shards(): pl.pallas_call(kernel, out_shape=jax.ShapeDtypeStruct((toks, width), bf16...  54.7 us
    unnamed x1, local copies, waits for them, and re-layouts  1.67 us

profile of v2, /device:TPU:32, one launch (start us, length us, event | category | flops | bytes accessed | tf_op | source)
XLA Modules:
  0.0 56.4 jit_solution(18122143492789821181)
XLA Ops:
  0.0 54.7 %shard_map.82 = bf16[64,2048]{1,0:T(8,128)(2,1)} custom-call(bf16[64,2048]{1,0:T(8,128)(2,1)} %tokens.1, bf16[16,2048]{1,0:T(8,128)(2,1)} %bitcast.2, bf16[1,2048,768]{2,1,0:T(8,128)(2,1)} %gate.1, bf16[1,2048,768]{2,1,0:T(8,128)(2,1)} %up.1, bf16[1,768,2048]{2,1,0:T(8,128)(2,1)} %down.1, s32[4,64]{1,0:T(4,128)} %bitcast.3, s32[1,256]{1,0:T(1,128)} %priority.1, ...), custom_call_target="tpu_custom_call" | custom-call | tf_op jit(solution)/shard_map/pallas_call | solution.py:302
  54.7 1.7 %copy.10 = bf16[64,2048]{1,0:T(8,128)(2,1)} copy(bf16[64,2048]{1,0:T(8,128)(2,1)} %shard_map.82) | data formatting | bytes 524288

commit v3 on v2

--- a/solution.py
+++ b/solution.py
@@ -30,7 +30,7 @@
 def kernel(
     tokens, router, gate, up, down, routing, priority, hot_list, out,
     grid_tok, part, relay, final, summed, relay2, final2, shares, columns,
-    w_gate, w_up, w_down, w_router, own, hidden, result, route_v, prio_v, hot_s,
+    w_gate, w_up, w_down, w_router, own, hidden, route_v, prio_v, hot_s,
     send_sem, recv_sem, local_sem, far_sem,
 ):
     me = lax.axis_index("expert")
@@ -209,16 +209,13 @@
             summed[3, s, HI] = total(summed[3, s, HI], relay2[s, 1]).astype(jnp.bfloat16)
             remote(("R-", s), summed.at[3, s, HI], final2.at[s, 1, HI], first[s][1])
 
-    out_copies = []
-
     def finish(s):
         got(("b+", 0, s), ("b-", 0, s), ("r+", 0, s), ("r-", 0, s))
         got(("B+", s), ("B-", s), ("R+", s), ("R-", s))
         at = pl.ds(s * half, half)
-        result[at] = total(
+        out[at] = total(
             part[0, s, 0], final[0, s, 0], final[0, s, 1], final2[s, 0], final2[s, 1]
         ).astype(jnp.bfloat16)
-        out_copies.append(local(result.at[at], out.at[at]))
 
     def make_shares():
         for made in own_in + small_in:
@@ -289,8 +286,6 @@
     assert len(landed) == len(copies)
     for made in copies.values():
         made.wait_send()
-    for made in out_copies:
-        made.wait()
 
 
 def shards(tokens, router_weight, gate_weight, up_weight, down_weight, routing, priority, hot_list):
@@ -303,7 +298,7 @@
         kernel,
         out_shape=jax.ShapeDtypeStruct((toks, width), bf16),
         in_specs=[hbm] * 8,
-        out_specs=hbm,
+        out_specs=pl.BlockSpec(memory_space=pltpu.VMEM),
         scratch_shapes=[
             pltpu.VMEM((SIDE, 2, SIDE, half, width), bf16),
             pltpu.VMEM((SIDE, 2, SIDE, half, width), bf16),
@@ -320,7 +315,6 @@
             pltpu.VMEM(router_weight.shape[::-1], bf16),
             pltpu.VMEM((2, half, width), bf16),
             pltpu.VMEM((SIDE * half, n_ff), bf16),
-            pltpu.VMEM((toks, width), bf16),
             pltpu.VMEM(routing.shape[::-1], jnp.int32),
             pltpu.VMEM(priority.shape, jnp.int32),
             pltpu.SMEM(hot_list.shape, jnp.int32),
@@ -330,11 +324,11 @@
             pltpu.SemaphoreType.REGULAR((2,)),
         ],
         compiler_params=pltpu.CompilerParams(
-            collective_id=0, has_side_effects=True, vmem_limit_bytes=67043328
+            collective_id=0, has_side_effects=True, vmem_limit_bytes=51683328
         ),
-    )(
+    )(*(pltpu.with_memory_space_constraint(v, pltpu.HBM) for v in (
         tokens, router_weight.T, gate_weight, up_weight, down_weight, routing.T, priority, hot_list
-    )
+    )))
 
 
 def solution(mesh):

time: 56.5 us -> 55.1 us (0.975)
  local copies, waits for them, and re-layouts: 1.67 us -> 0.71 us
    unnamed x1, local copies, waits for them, and re-layouts: 1.67 us -> 0.71 us
where the time goes in v3:
time: 55.1 us; the launch traced here: 55 us
  Pallas kernels  54.3 us (99%)
  local copies, waits for them, and re-layouts  0.71 us (1%)
    pallas_call x1, Pallas kernels, shards(): pl.pallas_call(kernel, out_shape=jax.ShapeDtypeStruct((toks, width), bf16...  54.3 us

profile of v3, /device:TPU:32, one launch (start us, length us, event | category | flops | bytes accessed | tf_op | source)
XLA Modules:
  0.0 55.0 jit_solution(5895572409803970939)
XLA Ops:
  0.0 54.3 %shard_map.82 = bf16[64,2048]{1,0:T(8,128)(2,1)S(1)} custom-call(bf16[64,2048]{1,0:T(8,128)(2,1)} %tokens.1, bf16[16,2048]{1,0:T(8,128)(2,1)} %bitcast.2, bf16[1,2048,768]{2,1,0:T(8,128)(2,1)} %gate.1, bf16[1,2048,768]{2,1,0:T(8,128)(2,1)} %up.1, bf16[1,768,2048]{2,1,0:T(8,128)(2,1)} %down.1, s32[4,64]{1,0:T(4,128)} %bitcast.3, s32[1,256]{1,0:T(1,128)} %priority.1, ...), custom_call_target="tpu_custom_call" | custom-call | tf_op jit(solution)/shard_map/pallas_call | solution.py:297
  54.3 0.7 %copy.10 = bf16[64,2048]{1,0:T(8,128)(2,1)} copy(bf16[64,2048]{1,0:T(8,128)(2,1)S(1)} %shard_map.82) | data formatting | bytes 524288

commit v4 on v3

--- a/solution.py
+++ b/solution.py
@@ -11,26 +11,27 @@
 N_SEMS = 128
 FAR = 4096.0
 ORDER = (
-    ("O", 1), ("O", 0), ("S", 0, 0), ("S", 0, 1), ("X",), ("f", 0, 1), ("f", 0, 0), ("f", 1, 0),
-    ("f", 1, 1), ("S", 3, 0), ("S", 3, 1), ("g", 1, 0, 0), ("g", 0, 0, 0), ("g", 0, 0, 1),
-    ("g", 1, 0, 1), ("Y",), ("S", 2, 1), ("S", 2, 0), ("g", 0, 3, 1), ("g", 1, 3, 1), ("g", 0, 3, 0),
-    ("g", 1, 3, 0), ("S", 1, 1), ("S", 1, 0), ("E", 0, 0), ("E", 0, 1), ("g", 1, 2, 1), ("g", 1, 2, 0),
-    ("g", 0, 2, 1), ("g", 0, 2, 0), ("E", 3, 1), ("b", 0, 1), ("b", 0, 0), ("E", 3, 0), ("b", 3, 1),
-    ("a", 3, 0), ("g", 0, 1, 1), ("g", 1, 1, 1), ("g", 0, 1, 0), ("g", 1, 1, 0), ("E", 2, 1),
-    ("b", 2, 1), ("E", 2, 0), ("b", 2, 0), ("a", 2, 0), ("a", 2, 1), ("r", 0, 3, 0), ("a", 3, 1),
-    ("r", 1, 3, 0), ("E", 1, 1), ("a", 1, 1), ("E", 1, 0), ("a", 1, 0), ("b", 3, 0), ("r", 0, 2, 1),
-    ("r", 1, 2, 1), ("b", 1, 1), ("r", 0, 2, 0), ("r", 1, 2, 0), ("r", 0, 3, 1), ("r", 1, 3, 1),
-    ("b", 1, 0), ("r", 0, 1, 1), ("r", 1, 1, 1), ("r", 0, 1, 0), ("r", 1, 1, 0), ("F", 2, 1), ("A", 1),
-    ("F", 3, 0), ("a", 0, 1), ("F", 2, 0), ("A", 0), ("a", 0, 0), ("F", 3, 1), ("B", 0, 0), ("B", 0, 1),
-    ("F", 1, 1), ("B", 1, 1), ("F", 1, 0), ("B", 1, 0), ("r", 0, 0, 1), ("r", 1, 0, 1), ("R", 0, 1),
-    ("R", 1, 1), ("R", 0, 0), ("R", 1, 0), ("r", 0, 0, 0), ("r", 1, 0, 0), ("Z", 1), ("Z", 0),
+    ("O", 0), ("O", 1), ("S", 0, 1), ("S", 0, 0), ("f", 0, 0), ("f", 1, 0), ("f", 1, 1), ("f", 0, 1),
+    ("S", 1, 1), ("S", 1, 0), ("X",), ("S", 2, 0), ("S", 2, 1), ("g", 1, 1, 0), ("g", 0, 1, 0),
+    ("S", 3, 1), ("Y",), ("g", 1, 1, 1), ("g", 0, 1, 1), ("S", 3, 0), ("g", 0, 0, 0), ("g", 0, 2, 1),
+    ("g", 1, 2, 0), ("g", 1, 2, 1), ("g", 0, 2, 0), ("g", 1, 0, 0), ("g", 0, 3, 1), ("g", 1, 3, 1),
+    ("E", 1, 0), ("g", 1, 0, 1), ("g", 0, 0, 1), ("b", 1, 0), ("E", 1, 1), ("b", 1, 1), ("g", 0, 3, 0),
+    ("a", 1, 0), ("E", 2, 1), ("g", 1, 3, 0), ("a", 2, 1), ("E", 2, 0), ("a", 1, 1), ("a", 2, 0),
+    ("b", 2, 0), ("E", 3, 1), ("a", 3, 1), ("b", 3, 1), ("r", 1, 2, 1), ("r", 1, 1, 0), ("r", 0, 1, 0),
+    ("b", 2, 1), ("r", 0, 2, 1), ("E", 3, 0), ("r", 1, 1, 1), ("a", 3, 0), ("r", 0, 2, 0),
+    ("r", 0, 1, 1), ("r", 1, 2, 0), ("E", 0, 0), ("E", 0, 1), ("a", 0, 0), ("r", 0, 3, 1), ("a", 0, 1),
+    ("b", 3, 0), ("r", 0, 3, 0), ("F", 1, 0), ("r", 1, 3, 0), ("F", 2, 1), ("r", 1, 3, 1), ("A", 1),
+    ("F", 2, 0), ("A", 0), ("B", 1, 0), ("r", 0, 0, 0), ("b", 0, 1), ("F", 1, 1), ("b", 0, 0),
+    ("r", 0, 0, 1), ("F", 3, 1), ("B", 1, 1), ("F", 3, 0), ("r", 1, 0, 1), ("r", 1, 0, 0), ("R", 0, 0),
+    ("B", 0, 1), ("B", 0, 0), ("R", 1, 1), ("R", 1, 0), ("R", 0, 1), ("P", 1), ("P", 0), ("Z", 0),
+    ("Z", 1),
 )
 
 
 def kernel(
     tokens, router, gate, up, down, routing, priority, hot_list, out,
     grid_tok, part, relay, final, summed, relay2, final2, shares, columns,
-    w_gate, w_up, w_down, w_router, own, hidden, route_v, prio_v, hot_s,
+    w_gate, w_up, w_down, w_router, own, mine, hidden, route_v, prio_v, hot_s,
     send_sem, recv_sem, local_sem, far_sem,
 ):
     me = lax.axis_index("expert")
@@ -82,19 +83,23 @@
     ]
     pl.semaphore_wait(barrier, 4)
 
+    def settle(left, keep):
+        while len(left) > keep:
+            left.pop(0).wait_send()
+
     def own_first(s):
-        mine = tokens.at[pl.ds(s * half, half)]
-        remote(("O+", s), mine, grid_tok.at[3, s, 0], first[s][0])
-        remote(("O-", s), mine, grid_tok.at[1, s, 0], first[s][1])
+        block = tokens.at[pl.ds(s * half, half)]
+        remote(("O+", s), block, grid_tok.at[3, s, 0], first[s][0])
+        remote(("O-", s), block, grid_tok.at[1, s, 0], first[s][1])
 
     def spread(d, s):
         if d == 0:
-            mine = tokens.at[pl.ds(s * half, half)]
+            block = tokens.at[pl.ds(s * half, half)]
         else:
             got(*{3: [("O+", s)], 1: [("O-", s)], 2: [("f+", s), ("f-", s)]}[d])
-            mine = grid_tok.at[d, s, 0]
-        remote(("S+", d, s), mine, grid_tok.at[d, s, 3], second[s][0])
-        remote(("S-", d, s), mine, grid_tok.at[d, s, 1], second[s][1])
+            block = grid_tok.at[d, s, 0]
+        remote(("S+", d, s), block, grid_tok.at[d, s, 3], second[s][0])
+        remote(("S-", d, s), block, grid_tok.at[d, s, 1], second[s][1])
 
     def pass_first(plus, s):
         if plus:
@@ -209,13 +214,13 @@
             summed[3, s, HI] = total(summed[3, s, HI], relay2[s, 1]).astype(jnp.bfloat16)
             remote(("R-", s), summed.at[3, s, HI], final2.at[s, 1, HI], first[s][1])
 
+    def fold_own(s):
+        got(("b+", 0, s), ("b-", 0, s), ("r+", 0, s), ("r-", 0, s))
+        mine[s] = total(part[0, s, 0], final[0, s, 0], final[0, s, 1])
+
     def finish(s):
-        got(("b+", 0, s), ("b-", 0, s), ("r+", 0, s), ("r-", 0, s))
         got(("B+", s), ("B-", s), ("R+", s), ("R-", s))
-        at = pl.ds(s * half, half)
-        out[at] = total(
-            part[0, s, 0], final[0, s, 0], final[0, s, 1], final2[s, 0], final2[s, 1]
-        ).astype(jnp.bfloat16)
+        out[pl.ds(s * half, half)] = total(mine[s], final2[s, 0], final2[s, 1]).astype(jnp.bfloat16)
 
     def make_shares():
         for made in own_in + small_in:
@@ -265,9 +270,9 @@
     run = {
         "O": own_first, "S": spread, "f": pass_first, "g": pass_second, "X": share_x, "Y": share_y,
         "E": expert, "a": far_halves, "b": near_halves, "r": add_second, "F": fold, "A": far_first,
-        "B": near_first, "R": add_first, "Z": finish,
+        "B": near_first, "R": add_first, "P": fold_own, "Z": finish,
     }
-    heavy_in = []
+    heavy_in, left = [], []
     for at, step in enumerate(ORDER):
         if at == 4:
             pl.semaphore_signal(
@@ -282,10 +287,14 @@
             heavy_in += [
                 local(gate.at[0], w_gate), local(up.at[0], w_up), local(down.at[0], w_down)
             ]
+        before = len(copies)
+        if step[0] == "P":
+            settle(left, 12)
         run[step[0]](*step[1:])
+        left += list(copies.values())[before:]
+        settle(left, 40)
     assert len(landed) == len(copies)
-    for made in copies.values():
-        made.wait_send()
+    settle(left, 0)
 
 
 def shards(tokens, router_weight, gate_weight, up_weight, down_weight, routing, priority, hot_list):
@@ -314,6 +323,7 @@
             pltpu.VMEM((n_ff, width), bf16),
             pltpu.VMEM(router_weight.shape[::-1], bf16),
             pltpu.VMEM((2, half, width), bf16),
+            pltpu.VMEM((2, half, width), f32),
             pltpu.VMEM((SIDE * half, n_ff), bf16),
             pltpu.VMEM(routing.shape[::-1], jnp.int32),
             pltpu.VMEM(priority.shape, jnp.int32),

time: 55.1 us -> 53.2 us (0.966)
  Pallas kernels: 54.3 us -> 52.5 us
    pallas_call x1, Pallas kernels: 54.3 us -> 52.5 us  [shards(): pl.pallas_call(kernel, out_shape=jax.ShapeDtypeStruct((toks, width), bf16...]
where the time goes in v4:
time: 53.2 us
  Pallas kernels  52.5 us (99%)
  local copies, waits for them, and re-layouts  0.71 us (1%)
    pallas_call x1, Pallas kernels, shards(): pl.pallas_call(kernel, out_shape=jax.ShapeDtypeStruct((toks, width), bf16...  52.5 us

profile of v4, /device:TPU:32, one launch (start us, length us, event | category | flops | bytes accessed | tf_op | source)
XLA Modules:
  0.0 53.2 jit_solution(14450091411018667209)
XLA Ops:
  0.0 52.5 %shard_map.82 = bf16[64,2048]{1,0:T(8,128)(2,1)S(1)} custom-call(bf16[64,2048]{1,0:T(8,128)(2,1)} %tokens.1, bf16[16,2048]{1,0:T(8,128)(2,1)} %bitcast.2, bf16[1,2048,768]{2,1,0:T(8,128)(2,1)} %gate.1, bf16[1,2048,768]{2,1,0:T(8,128)(2,1)} %up.1, bf16[1,768,2048]{2,1,0:T(8,128)(2,1)} %down.1, s32[4,64]{1,0:T(4,128)} %bitcast.3, s32[1,256]{1,0:T(1,128)} %priority.1, ...), custom_call_target="tpu_custom_call" | custom-call | tf_op jit(solution)/shard_map/pallas_call | solution.py:306
  52.5 0.7 %copy.10 = bf16[64,2048]{1,0:T(8,128)(2,1)} copy(bf16[64,2048]{1,0:T(8,128)(2,1)S(1)} %shard_map.82) | data formatting | bytes 524288

commit v5 on v4

--- a/solution.py
+++ b/solution.py
@@ -11,20 +11,20 @@
 N_SEMS = 128
 FAR = 4096.0
 ORDER = (
-    ("O", 0), ("O", 1), ("S", 0, 1), ("S", 0, 0), ("f", 0, 0), ("f", 1, 0), ("f", 1, 1), ("f", 0, 1),
-    ("S", 1, 1), ("S", 1, 0), ("X",), ("S", 2, 0), ("S", 2, 1), ("g", 1, 1, 0), ("g", 0, 1, 0),
-    ("S", 3, 1), ("Y",), ("g", 1, 1, 1), ("g", 0, 1, 1), ("S", 3, 0), ("g", 0, 0, 0), ("g", 0, 2, 1),
-    ("g", 1, 2, 0), ("g", 1, 2, 1), ("g", 0, 2, 0), ("g", 1, 0, 0), ("g", 0, 3, 1), ("g", 1, 3, 1),
-    ("E", 1, 0), ("g", 1, 0, 1), ("g", 0, 0, 1), ("b", 1, 0), ("E", 1, 1), ("b", 1, 1), ("g", 0, 3, 0),
-    ("a", 1, 0), ("E", 2, 1), ("g", 1, 3, 0), ("a", 2, 1), ("E", 2, 0), ("a", 1, 1), ("a", 2, 0),
-    ("b", 2, 0), ("E", 3, 1), ("a", 3, 1), ("b", 3, 1), ("r", 1, 2, 1), ("r", 1, 1, 0), ("r", 0, 1, 0),
-    ("b", 2, 1), ("r", 0, 2, 1), ("E", 3, 0), ("r", 1, 1, 1), ("a", 3, 0), ("r", 0, 2, 0),
-    ("r", 0, 1, 1), ("r", 1, 2, 0), ("E", 0, 0), ("E", 0, 1), ("a", 0, 0), ("r", 0, 3, 1), ("a", 0, 1),
-    ("b", 3, 0), ("r", 0, 3, 0), ("F", 1, 0), ("r", 1, 3, 0), ("F", 2, 1), ("r", 1, 3, 1), ("A", 1),
-    ("F", 2, 0), ("A", 0), ("B", 1, 0), ("r", 0, 0, 0), ("b", 0, 1), ("F", 1, 1), ("b", 0, 0),
-    ("r", 0, 0, 1), ("F", 3, 1), ("B", 1, 1), ("F", 3, 0), ("r", 1, 0, 1), ("r", 1, 0, 0), ("R", 0, 0),
-    ("B", 0, 1), ("B", 0, 0), ("R", 1, 1), ("R", 1, 0), ("R", 0, 1), ("P", 1), ("P", 0), ("Z", 0),
-    ("Z", 1),
+    ("O", 0), ("O", 1), ("S", 0, 1), ("S", 0, 0), ("X",), ("S", 3, 0), ("S", 1, 1), ("f", 1, 1),
+    ("f", 1, 0), ("f", 0, 0), ("g", 0, 0, 1), ("f", 0, 1), ("Y",), ("g", 1, 0, 1), ("S", 1, 0),
+    ("g", 1, 3, 0), ("g", 0, 3, 0), ("g", 0, 1, 1), ("g", 1, 1, 1), ("S", 2, 1), ("S", 3, 1),
+    ("S", 2, 0), ("E", 0, 1), ("g", 1, 1, 0), ("g", 1, 0, 0), ("g", 0, 1, 0), ("E", 1, 1),
+    ("g", 0, 2, 1), ("g", 1, 2, 1), ("a", 1, 1), ("a", 0, 1), ("g", 0, 0, 0), ("E", 3, 0),
+    ("g", 0, 2, 0), ("g", 1, 2, 0), ("a", 3, 0), ("b", 3, 0), ("g", 1, 3, 1), ("b", 1, 1),
+    ("g", 0, 3, 1), ("E", 1, 0), ("b", 1, 0), ("a", 1, 0), ("E", 2, 1), ("a", 2, 1), ("b", 2, 1),
+    ("E", 2, 0), ("a", 2, 0), ("r", 0, 0, 1), ("r", 1, 1, 1), ("b", 2, 0), ("E", 3, 1), ("a", 3, 1),
+    ("r", 1, 3, 0), ("r", 1, 2, 1), ("r", 0, 3, 0), ("r", 1, 0, 1), ("r", 0, 2, 1), ("r", 0, 1, 1),
+    ("r", 0, 2, 0), ("r", 1, 2, 0), ("r", 1, 1, 0), ("b", 3, 1), ("r", 0, 1, 0), ("E", 0, 0),
+    ("a", 0, 0), ("r", 1, 3, 1), ("r", 0, 3, 1), ("F", 2, 1), ("A", 1), ("F", 2, 0), ("A", 0),
+    ("b", 0, 0), ("F", 1, 1), ("F", 3, 0), ("B", 0, 0), ("b", 0, 1), ("B", 1, 1), ("r", 0, 0, 0),
+    ("F", 1, 0), ("B", 1, 0), ("r", 1, 0, 0), ("F", 3, 1), ("R", 0, 1), ("R", 1, 1), ("R", 0, 0),
+    ("R", 1, 0), ("B", 0, 1), ("P", 1), ("P", 0), ("Z", 0), ("Z", 1),
 )
 
 

time: 53.2 us -> 52.6 us (0.989)
  Pallas kernels: 52.5 us -> 51.8 us
    pallas_call x1, Pallas kernels: 52.5 us -> 51.8 us  [shards(): pl.pallas_call(kernel, out_shape=jax.ShapeDtypeStruct((toks, width), bf16...]
where the time goes in v5:
time: 52.6 us; the launch traced here: 52.5 us
  Pallas kernels  51.8 us (98%)
  local copies, waits for them, and re-layouts  0.71 us (1%)
    pallas_call x1, Pallas kernels, shards(): pl.pallas_call(kernel, out_shape=jax.ShapeDtypeStruct((toks, width), bf16...  51.8 us

profile of v5, /device:TPU:32, one launch (start us, length us, event | category | flops | bytes accessed | tf_op | source)
XLA Modules:
  0.0 52.5 jit_solution(15997950330341492481)
XLA Ops:
  0.0 51.8 %shard_map.82 = bf16[64,2048]{1,0:T(8,128)(2,1)S(1)} custom-call(bf16[64,2048]{1,0:T(8,128)(2,1)} %tokens.1, bf16[16,2048]{1,0:T(8,128)(2,1)} %bitcast.2, bf16[1,2048,768]{2,1,0:T(8,128)(2,1)} %gate.1, bf16[1,2048,768]{2,1,0:T(8,128)(2,1)} %up.1, bf16[1,768,2048]{2,1,0:T(8,128)(2,1)} %down.1, s32[4,64]{1,0:T(4,128)} %bitcast.3, s32[1,256]{1,0:T(1,128)} %priority.1, ...), custom_call_target="tpu_custom_call" | custom-call | tf_op jit(solution)/shard_map/pallas_call | solution.py:306
  51.8 0.7 %copy.10 = bf16[64,2048]{1,0:T(8,128)(2,1)} copy(bf16[64,2048]{1,0:T(8,128)(2,1)S(1)} %shard_map.82) | data formatting | bytes 524288

commit v6 on v5

--- a/solution.py
+++ b/solution.py
@@ -14,17 +14,18 @@
     ("O", 0), ("O", 1), ("S", 0, 1), ("S", 0, 0), ("X",), ("S", 3, 0), ("S", 1, 1), ("f", 1, 1),
     ("f", 1, 0), ("f", 0, 0), ("g", 0, 0, 1), ("f", 0, 1), ("Y",), ("g", 1, 0, 1), ("S", 1, 0),
     ("g", 1, 3, 0), ("g", 0, 3, 0), ("g", 0, 1, 1), ("g", 1, 1, 1), ("S", 2, 1), ("S", 3, 1),
-    ("S", 2, 0), ("E", 0, 1), ("g", 1, 1, 0), ("g", 1, 0, 0), ("g", 0, 1, 0), ("E", 1, 1),
-    ("g", 0, 2, 1), ("g", 1, 2, 1), ("a", 1, 1), ("a", 0, 1), ("g", 0, 0, 0), ("E", 3, 0),
-    ("g", 0, 2, 0), ("g", 1, 2, 0), ("a", 3, 0), ("b", 3, 0), ("g", 1, 3, 1), ("b", 1, 1),
-    ("g", 0, 3, 1), ("E", 1, 0), ("b", 1, 0), ("a", 1, 0), ("E", 2, 1), ("a", 2, 1), ("b", 2, 1),
-    ("E", 2, 0), ("a", 2, 0), ("r", 0, 0, 1), ("r", 1, 1, 1), ("b", 2, 0), ("E", 3, 1), ("a", 3, 1),
-    ("r", 1, 3, 0), ("r", 1, 2, 1), ("r", 0, 3, 0), ("r", 1, 0, 1), ("r", 0, 2, 1), ("r", 0, 1, 1),
-    ("r", 0, 2, 0), ("r", 1, 2, 0), ("r", 1, 1, 0), ("b", 3, 1), ("r", 0, 1, 0), ("E", 0, 0),
-    ("a", 0, 0), ("r", 1, 3, 1), ("r", 0, 3, 1), ("F", 2, 1), ("A", 1), ("F", 2, 0), ("A", 0),
-    ("b", 0, 0), ("F", 1, 1), ("F", 3, 0), ("B", 0, 0), ("b", 0, 1), ("B", 1, 1), ("r", 0, 0, 0),
-    ("F", 1, 0), ("B", 1, 0), ("r", 1, 0, 0), ("F", 3, 1), ("R", 0, 1), ("R", 1, 1), ("R", 0, 0),
-    ("R", 1, 0), ("B", 0, 1), ("P", 1), ("P", 0), ("Z", 0), ("Z", 1),
+    ("S", 2, 0), ("E", 0, 1), ("D", 0, 1), ("g", 1, 1, 0), ("g", 1, 0, 0), ("g", 0, 1, 0), ("E", 1, 1),
+    ("D", 1, 1), ("g", 0, 2, 1), ("g", 1, 2, 1), ("a", 1, 1), ("a", 0, 1), ("g", 0, 0, 0), ("E", 3, 0),
+    ("D", 3, 0), ("g", 0, 2, 0), ("g", 1, 2, 0), ("a", 3, 0), ("b", 3, 0), ("g", 1, 3, 1), ("b", 1, 1),
+    ("g", 0, 3, 1), ("E", 1, 0), ("D", 1, 0), ("b", 1, 0), ("a", 1, 0), ("E", 2, 1), ("D", 2, 1),
+    ("a", 2, 1), ("b", 2, 1), ("E", 2, 0), ("D", 2, 0), ("a", 2, 0), ("r", 0, 0, 1), ("r", 1, 1, 1),
+    ("b", 2, 0), ("E", 3, 1), ("D", 3, 1), ("a", 3, 1), ("r", 1, 3, 0), ("r", 1, 2, 1), ("r", 0, 3, 0),
+    ("r", 1, 0, 1), ("r", 0, 2, 1), ("r", 0, 1, 1), ("r", 0, 2, 0), ("r", 1, 2, 0), ("r", 1, 1, 0),
+    ("b", 3, 1), ("r", 0, 1, 0), ("E", 0, 0), ("D", 0, 0), ("a", 0, 0), ("r", 1, 3, 1), ("r", 0, 3, 1),
+    ("F", 2, 1), ("A", 1), ("F", 2, 0), ("A", 0), ("b", 0, 0), ("F", 1, 1), ("F", 3, 0), ("B", 0, 0),
+    ("b", 0, 1), ("B", 1, 1), ("r", 0, 0, 0), ("F", 1, 0), ("B", 1, 0), ("r", 1, 0, 0), ("F", 3, 1),
+    ("R", 0, 1), ("R", 1, 1), ("R", 0, 0), ("R", 1, 0), ("B", 0, 1), ("P", 1), ("P", 0), ("Z", 0),
+    ("Z", 1),
 )
 
 
@@ -135,14 +136,22 @@
     rows = SIDE * half
     loaded = []
 
-    def expert(d, s):
+    def hidden_block(d, s):
         if not loaded:
-            got("X+", "X-", "X2", "Y+", "Y-", "Y2")
             for made in heavy_in:
                 made.wait()
             loaded.append(1)
         got(("S+", d, s), ("S-", d, s), ("g+", d, s), ("g-", d, s))
         got(*{0: [], 3: [("O+", s)], 1: [("O-", s)], 2: [("f+", s), ("f-", s)]}[d])
+        block = grid_tok[d, s].reshape(rows, width)
+        for n in range(n_ff // 256):
+            at = pl.ds(n * 256, 256)
+            g = jnp.dot(block, w_gate[:, at], preferred_element_type=jnp.float32)
+            u = jnp.dot(block, w_up[:, at], preferred_element_type=jnp.float32)
+            hidden[d, s, :, at] = (g / (1.0 + jnp.exp(-g)) * u).astype(jnp.bfloat16)
+
+    def answer_block(d, s):
+        got("X+", "X-", "X2", "Y+", "Y-", "Y2")
         share_row = lax.broadcasted_iota(jnp.int32, (8, 128), 0) == my_row
         token_lane = lax.broadcasted_iota(jnp.int32, (half, 128), 1)
         token_row = lax.broadcasted_iota(jnp.int32, (half, 128), 0)
@@ -154,15 +163,9 @@
             columns[pl.ds(e * half, half)] = jnp.broadcast_to(
                 jnp.sum(jnp.where(pick, row, 0.0), axis=1, keepdims=True), (half, 128)
             )
-        for n in range(n_ff // 256):
-            at = pl.ds(n * 256, 256)
-            block = grid_tok[d, s].reshape(rows, width)
-            g = jnp.dot(block, w_gate[:, at], preferred_element_type=jnp.float32)
-            u = jnp.dot(block, w_up[:, at], preferred_element_type=jnp.float32)
-            hidden[:, at] = (g / (1.0 + jnp.exp(-g)) * u).astype(jnp.bfloat16)
         for n in range(width // 256):
             at = pl.ds(n * 256, 256)
-            o = jnp.dot(hidden[...], w_down[:, at], preferred_element_type=jnp.float32)
+            o = jnp.dot(hidden[d, s], w_down[:, at], preferred_element_type=jnp.float32)
             scale = jnp.concatenate([columns[...], columns[...]], axis=1)
             part[d, s, :, :, at] = (o * scale).astype(jnp.bfloat16).reshape(SIDE, half, 256)
 
@@ -269,7 +272,7 @@
 
     run = {
         "O": own_first, "S": spread, "f": pass_first, "g": pass_second, "X": share_x, "Y": share_y,
-        "E": expert, "a": far_halves, "b": near_halves, "r": add_second, "F": fold, "A": far_first,
+        "E": hidden_block, "D": answer_block, "a": far_halves, "b": near_halves, "r": add_second, "F": fold, "A": far_first,
         "B": near_first, "R": add_first, "P": fold_own, "Z": finish,
     }
     heavy_in, left = [], []
@@ -324,7 +327,7 @@
             pltpu.VMEM(router_weight.shape[::-1], bf16),
             pltpu.VMEM((2, half, width), bf16),
             pltpu.VMEM((2, half, width), f32),
-            pltpu.VMEM((SIDE * half, n_ff), bf16),
+            pltpu.VMEM((SIDE, 2, SIDE * half, n_ff), bf16),
             pltpu.VMEM(routing.shape[::-1], jnp.int32),
             pltpu.VMEM(priority.shape, jnp.int32),
             pltpu.SMEM(hot_list.shape, jnp.int32),

time: 52.6 us -> 52.6 us (level)
  no operation moved by 1% of the time
where the time goes in v6:
time: 52.6 us; the launch traced here: 52.5 us
  Pallas kernels  51.8 us (98%)
  local copies, waits for them, and re-layouts  0.71 us (1%)
    pallas_call x1, Pallas kernels, shards(): pl.pallas_call(kernel, out_shape=jax.ShapeDtypeStruct((toks, width), bf16...  51.8 us

profile of v6, /device:TPU:32, one launch (start us, length us, event | category | flops | bytes accessed | tf_op | source)
XLA Modules:
  0.0 52.5 jit_solution(9199428397014590980)
XLA Ops:
  0.0 51.8 %shard_map.82 = bf16[64,2048]{1,0:T(8,128)(2,1)S(1)} custom-call(bf16[64,2048]{1,0:T(8,128)(2,1)} %tokens.1, bf16[16,2048]{1,0:T(8,128)(2,1)} %bitcast.2, bf16[1,2048,768]{2,1,0:T(8,128)(2,1)} %gate.1, bf16[1,2048,768]{2,1,0:T(8,128)(2,1)} %up.1, bf16[1,768,2048]{2,1,0:T(8,128)(2,1)} %down.1, s32[4,64]{1,0:T(4,128)} %bitcast.3, s32[1,256]{1,0:T(1,128)} %priority.1, ...), custom_call_target="tpu_custom_call" | custom-call | tf_op jit(solution)/shard_map/pallas_call | solution.py:309
  51.8 0.7 %copy.10 = bf16[64,2048]{1,0:T(8,128)(2,1)} copy(bf16[64,2048]{1,0:T(8,128)(2,1)S(1)} %shard_map.82) | data formatting | bytes 524288
